TPU v7x, 128 devices: a whole 4x4x4 slice. The times are simulated.
128 devices in a mesh: row: 8 (over y, core), col: 16 (over z, x).
Axes of the slice: x: 4, y: 4, z: 4, core: 2. Of those that a mesh axis runs over, the one named last changes fastest.
Arguments:
- child_fronts: float32 [2, 8192, 8192], P(None, 'row', 'col'), as said below
- parent_front: float32 [12288, 12288], P('row', 'col'), as said below
- child_map: int32 [2, 7168], replicated, may hold values from 0 to 12287, as said below
Outputs:
- child_factor: float32 [2, 8192, 1024], P(None, 'row', 'col')
- parent_factor: float32 [12288, 256], P('row', 'col')
- parent_schur: float32 [12288, 12288], P('row', 'col')
Inputs may be any that keep to these rules, and one draw needn't show every extreme that they name: child_fronts[k] and parent_front are symmetric positive definite. parent_front is symmetric positive definite. The entries of child_map[k] are distinct. Each aligned block of 512 entries of child_map[k] names exactly 32 indices in each aligned block of 768 parent indices.
All inputs are finite; a program needn't handle non-finite values.
Results may differ from a plain program's by a relative error of at most 0.0003.
Values sent between devices are 32-bit elements; how exact they have to be, the bound alone decides.
No kernel may reach another device: no remote copies, remote signals or barrier semaphores. Data moves between devices by JAX's collectives and lax.ppermute only.
A program may use at most 192 MiB of HBM per device.

v0:
```python
from functools import partial
import jax
import jax.numpy as jnp
from jax import lax
from jax.sharding import PartitionSpec as P

PP = 256
NB = 256
exact_mode = lax.Precision.HIGHEST


def from_root(value, axis, source):
    kept = jnp.where(lax.axis_index(axis) == source, value, 0).astype(value.dtype)
    return lax.psum(kept, axis)


def outer_update(factor_rows, crossed):
    return jnp.einsum("kin,kjn->kij", factor_rows, crossed, precision=exact_mode)


def take_rows(block, order):
    return jax.vmap(lambda single, picks: jnp.take(single, picks, axis=0))(block, order)


def take_both(block, row_order, col_order):
    rows_first = take_rows(block, row_order)
    flipped = take_rows(jnp.swapaxes(rows_first, 1, 2), col_order)
    return jnp.swapaxes(flipped, 1, 2)


def eliminate(tiles, pivots, send_panel, send_corner, send_cross):
    members, tile_rows, tile_cols = tiles.shape
    row_index = lax.axis_index("row")
    col_index = lax.axis_index("col")
    global_rows = row_index * tile_rows + jnp.arange(tile_rows, dtype=jnp.int32)
    total_steps = pivots // NB
    identity = jnp.broadcast_to(jnp.eye(NB, dtype=jnp.float32), (members, NB, NB))
    collected = []
    current = send_panel(lax.slice_in_dim(tiles, 0, NB, axis=2), 0)
    for panel_step in range(total_steps):
        offset = panel_step * NB
        owner_row = offset // tile_rows
        within_row = offset - owner_row * tile_rows
        corner = send_corner(
            lax.slice_in_dim(current, within_row, within_row + NB, axis=1), owner_row
        )
        factor = jnp.linalg.cholesky(corner)
        inverse = jax.vmap(partial(jax.scipy.linalg.solve_triangular, lower=True))(factor, identity)
        solved = jnp.einsum("krn,kmn->krm", current, inverse, precision=exact_mode)
        factor_rows = jnp.where((global_rows >= offset)[None, :, None], solved, jnp.float32(0.0))
        cross_first = col_index * tile_cols
        cross_owner = cross_first // tile_rows
        local_first = jnp.clip(cross_first - row_index * tile_rows, 0, tile_rows - tile_cols)
        crossed = send_cross(
            lax.dynamic_slice_in_dim(factor_rows, local_first, tile_cols, axis=1), cross_owner
        )
        collected.append(factor_rows)
        if panel_step + 1 < total_steps:
            upcoming = offset + NB
            next_owner = upcoming // tile_cols
            next_within = upcoming - next_owner * tile_cols
            tiles = tiles - outer_update(factor_rows, crossed)
            current = send_panel(
                lax.slice_in_dim(tiles, next_within, next_within + NB, axis=2), next_owner
            )
        else:
            tiles = tiles - outer_update(factor_rows, crossed)
    return (tiles, jnp.concatenate(collected, axis=2))


def inverse_list(targets, length, filler):
    sources = jnp.arange(targets.shape[0], dtype=jnp.int32)
    start = jnp.full((length,), filler, jnp.int32)
    return start.at[targets].set(sources, mode="drop")


def extend_add(tiles, child_map, parent_front):
    members, tile_rows, tile_cols = tiles.shape
    row_count = lax.axis_size("row")
    col_count = lax.axis_size("col")
    row_index = lax.axis_index("row")
    col_index = lax.axis_index("col")
    width = tile_rows * row_count
    pivots = width - child_map.shape[1]
    parent_rows = parent_front.shape[0]
    parent_cols = parent_front.shape[1]
    row_slots = tile_rows // row_count
    col_slots = tile_cols // col_count
    full_map = jnp.concatenate([jnp.zeros((members, pivots), jnp.int32), child_map], axis=1)
    positions = jnp.arange(width, dtype=jnp.int32)[None, :]
    row_keys = jnp.where(positions < pivots, row_count, full_map // parent_rows)
    col_keys = jnp.where(positions < pivots, col_count, full_map // parent_cols)
    row_orders = jnp.argsort(row_keys.reshape(members, row_count, tile_rows), axis=2, stable=True)
    col_orders = jnp.argsort(col_keys.reshape(members, col_count, tile_cols), axis=2, stable=True)
    row_blocks = jnp.arange(row_count, dtype=jnp.int32)
    col_blocks = jnp.arange(col_count, dtype=jnp.int32)
    row_live = jnp.clip((row_blocks + 1) * tile_rows - pivots, 0, tile_rows) // row_count
    col_live = jnp.clip((col_blocks + 1) * tile_cols - pivots, 0, tile_cols) // col_count
    row_seats = jnp.arange(row_slots, dtype=jnp.int32)
    col_seats = jnp.arange(col_slots, dtype=jnp.int32)
    own_row_live = row_live[row_index]
    send_row_pos = jnp.minimum(
        row_blocks[:, None] * own_row_live + row_seats[None, :], tile_rows - 1
    )
    send_row_keep = jnp.broadcast_to(
        row_seats[None, :] < own_row_live, (row_count, row_slots)
    ).reshape(-1)
    own_row_order = jnp.take(row_orders, row_index, axis=1)
    send_rows = jnp.take(own_row_order, send_row_pos.reshape(-1), axis=1)
    own_col_live = col_live[col_index]
    send_col_pos = jnp.minimum(
        col_blocks[:, None] * own_col_live + col_seats[None, :], tile_cols - 1
    )
    send_col_keep = jnp.broadcast_to(
        col_seats[None, :] < own_col_live, (col_count, col_slots)
    ).reshape(-1)
    own_col_order = jnp.take(col_orders, col_index, axis=1)
    send_cols = jnp.take(own_col_order, send_col_pos.reshape(-1), axis=1)
    picked = take_both(tiles, send_rows, send_cols)
    picked = jnp.where(
        send_row_keep[None, :, None] & send_col_keep[None, None, :], picked, jnp.float32(0.0)
    )
    outgoing = jnp.transpose(
        picked.reshape(members, row_count, row_slots, col_count, col_slots), (1, 3, 0, 2, 4)
    )
    flat = outgoing.reshape(row_count * col_count, members, row_slots, col_slots)
    arrived = lax.all_to_all(flat, ("row", "col"), split_axis=0, concat_axis=0, tiled=True)
    arrived = arrived.reshape(row_count, col_count, members, row_slots, col_slots)
    received = jnp.transpose(arrived, (2, 0, 3, 1, 4)).reshape(members, tile_rows, tile_cols)
    recv_row_pos = jnp.minimum(row_index * row_live[:, None] + row_seats[None, :], tile_rows - 1)
    recv_row_keep = (row_seats[None, :] < row_live[:, None]).reshape(-1)
    local_rows = jnp.take_along_axis(row_orders, recv_row_pos[None, :, :], axis=2)
    global_rows = (row_blocks[None, :, None] * tile_rows + local_rows).reshape(members, -1)
    target_rows = jnp.take_along_axis(full_map, global_rows, axis=1) - row_index * parent_rows
    target_rows = jnp.where(recv_row_keep[None, :], target_rows, parent_rows)
    recv_col_pos = jnp.minimum(col_index * col_live[:, None] + col_seats[None, :], tile_cols - 1)
    recv_col_keep = (col_seats[None, :] < col_live[:, None]).reshape(-1)
    local_cols = jnp.take_along_axis(col_orders, recv_col_pos[None, :, :], axis=2)
    global_cols = (col_blocks[None, :, None] * tile_cols + local_cols).reshape(members, -1)
    target_cols = jnp.take_along_axis(full_map, global_cols, axis=1) - col_index * parent_cols
    target_cols = jnp.where(recv_col_keep[None, :], target_cols, parent_cols)
    row_sources = jax.vmap(lambda targets: inverse_list(targets, parent_rows, tile_rows))(
        target_rows
    )
    col_sources = jax.vmap(lambda targets: inverse_list(targets, parent_cols, tile_cols))(
        target_cols
    )
    padded = jnp.concatenate([received, jnp.zeros((members, 1, tile_cols), jnp.float32)], axis=1)
    placed_rows = take_rows(padded, row_sources)
    flipped = jnp.swapaxes(placed_rows, 1, 2)
    flipped = jnp.concatenate([flipped, jnp.zeros((members, 1, parent_rows), jnp.float32)], axis=1)
    placed = jnp.swapaxes(take_rows(flipped, col_sources), 1, 2)
    merged = parent_front
    for which_child in range(members):
        merged = merged + placed[which_child]
    return merged


def child_panel(piece, owner):
    return from_root(piece, "col", owner)


def child_corner(piece, owner):
    return from_root(piece, "row", owner)


def child_cross(piece, owner):
    return from_root(piece, "row", owner)


def parent_panel(piece, owner):
    return from_root(piece, "col", owner)


def parent_corner(piece, owner):
    return from_root(piece, "row", owner)


def parent_cross(piece, owner):
    return from_root(piece, "row", owner)


def local(child_fronts, parent_front, child_map):
    col_count = lax.axis_size("col")
    row_index = lax.axis_index("row")
    col_index = lax.axis_index("col")
    tile_rows = child_fronts.shape[1]
    width = tile_rows * lax.axis_size("row")
    pivots = width - child_map.shape[1]
    updated, child_panels = eliminate(child_fronts, pivots, child_panel, child_corner, child_cross)
    merged = extend_add(updated, child_map, parent_front)
    parent_updated, parent_panels = eliminate(
        merged[None], PP, parent_panel, parent_corner, parent_cross
    )
    child_share = pivots // col_count
    child_factor = lax.dynamic_slice_in_dim(
        child_panels, col_index * child_share, child_share, axis=2
    )
    parent_share = PP // col_count
    parent_factor = lax.dynamic_slice_in_dim(
        parent_panels[0], col_index * parent_share, parent_share, axis=1
    )
    parent_rows = parent_front.shape[0]
    parent_cols = parent_front.shape[1]
    global_rows = row_index * parent_rows + jnp.arange(parent_rows, dtype=jnp.int32)
    global_cols = col_index * parent_cols + jnp.arange(parent_cols, dtype=jnp.int32)
    keep = (global_rows[:, None] >= PP) & (global_cols[None, :] >= PP)
    parent_schur = jnp.where(keep, parent_updated[0], jnp.float32(0.0))
    return (child_factor, parent_factor, parent_schur)


def solution(mesh):
    placed = (P(None, "row", "col"), P("row", "col"), P())
    return jax.shard_map(
        local,
        mesh=mesh,
        in_specs=placed,
        out_specs=(P(None, "row", "col"), P("row", "col"), P("row", "col")),
        check_vma=False,
    )
```

profile of v0, /device:TPU:0, one launch (start us, length us, event | category | flops | bytes accessed | tf_op | source)
XLA Modules:
  0.0 2048.3 jit_solution(9405431235240546591)
XLA Ops:
  16.8 92.8 %all-reduce.21.cloned.1.call-done = f32[2,1024,256]{1,2,0:T(8,128)} async-done(((f32[2,1024,256]{1,2,0:T(8,128)}), f32[2,1024,256]{1,2,0:T(8,128)}) %all-reduce.21.cloned.1.call-update) | async-done | bytes 2097168 | tf_op jit(solution)/shard_map/psum | solution.py:14
  111.5 61.1 %all-reduce.23.cloned.1.call-done = f32[2,256,256]{1,2,0:T(8,128)} async-done(((f32[2,256,256]{1,2,0:T(8,128)}), f32[2,256,256]{1,2,0:T(8,128)}) %all-reduce.23.cloned.1.call-update) | async-done | bytes 524304 | tf_op jit(solution)/shard_map/psum | solution.py:14
  175.0 23.5 %custom-call.62 = f32[2,128,128]{2,1,0:T(8,128)S(1)} custom-call(f32[2,128,128]{2,1,0:T(8,128)S(1)} %cholesky.464), custom_call_target="Cholesky" | custom-call | tf_op jit(solution)/shard_map/jit(cholesky)/cholesky | solution.py:47
  198.5 19.7 custom-call.63
  218.9 23.5 %custom-call.64 = f32[2,128,128]{2,1,0:T(8,128)S(1)} custom-call(f32[2,128,128]{2,1,0:T(8,128)S(1)} %convolution_subtract_fusion.11), custom_call_target="Cholesky" | custom-call | tf_op jit(solution)/shard_map/jit(cholesky)/cholesky | solution.py:47
  246.8 39.5 %custom-call.65 = f32[2,2,128,128]{2,3,1,0:T(8,128)S(1)} custom-call(f32[2,2,128,128]{3,2,1,0:T(8,128)S(1)} %bitcast.389), custom_call_target="InvertDiagBlocksLowerTriangular" | custom-call | tf_op jit(solution)/shard_map/vmap(jit(_solve_triangular))/triangular_solve | solution.py:48
  292.8 61.7 %all-reduce.25.cloned.1.call-done = f32[2,512,256]{1,2,0:T(8,128)} async-done(((f32[2,512,256]{1,2,0:T(8,128)}), f32[2,512,256]{1,2,0:T(8,128)}) %all-reduce.25.cloned.1.call-update) | async-done | bytes 1048592 | tf_op jit(solution)/shard_map/psum | solution.py:14
  365.3 89.7 %all-reduce.27.cloned.1.call-done = f32[2,1024,256]{1,2,0:T(8,128)} async-done(((f32[2,1024,256]{1,2,0:T(8,128)}), f32[2,1024,256]{1,2,0:T(8,128)}) %all-reduce.27.cloned.1.call-update) | async-done | bytes 2097168 | tf_op jit(solution)/shard_map/psum | solution.py:14
  457.0 61.0 %all-reduce.29.cloned.1.call-done = f32[2,256,256]{1,2,0:T(8,128)} async-done(((f32[2,256,256]{1,2,0:T(8,128)}), f32[2,256,256]{1,2,0:T(8,128)}) %all-reduce.29.cloned.1.call-update) | async-done | bytes 524304 | tf_op jit(solution)/shard_map/psum | solution.py:14
  520.3 23.9 %custom-call.66 = f32[2,128,128]{2,1,0:T(8,128)S(1)} custom-call(f32[2,128,128]{2,1,0:T(8,128)S(1)} %cholesky.467), custom_call_target="Cholesky" | custom-call | tf_op jit(solution)/shard_map/jit(cholesky)/cholesky | solution.py:47
  564.6 23.5 %custom-call.68 = f32[2,128,128]{2,1,0:T(8,128)S(1)} custom-call(f32[2,128,128]{2,1,0:T(8,128)S(1)} %convolution_subtract_fusion.10), custom_call_target="Cholesky" | custom-call | tf_op jit(solution)/shard_map/jit(cholesky)/cholesky | solution.py:47
  592.5 39.5 %custom-call.69 = f32[2,2,128,128]{2,3,1,0:T(8,128)S(1)} custom-call(f32[2,2,128,128]{3,2,1,0:T(8,128)S(1)} %bitcast.390), custom_call_target="InvertDiagBlocksLowerTriangular" | custom-call | tf_op jit(solution)/shard_map/vmap(jit(_solve_triangular))/triangular_solve | solution.py:48
  638.6 61.7 %all-reduce.31.cloned.1.call-done = f32[2,512,256]{1,2,0:T(8,128)} async-done(((f32[2,512,256]{1,2,0:T(8,128)}), f32[2,512,256]{1,2,0:T(8,128)}) %all-reduce.31.cloned.1.call-update) | async-done | bytes 1048592 | tf_op jit(solution)/shard_map/psum | solution.py:14
  711.1 89.7 %all-reduce.33.cloned.1.call-done = f32[2,1024,256]{1,2,0:T(8,128)} async-done(((f32[2,1024,256]{1,2,0:T(8,128)}), f32[2,1024,256]{1,2,0:T(8,128)}) %all-reduce.33.cloned.1.call-update) | async-done | bytes 2097168 | tf_op jit(solution)/shard_map/psum | solution.py:14
  802.8 61.1 %all-reduce.35.cloned.1.call-done = f32[2,256,256]{1,2,0:T(8,128)} async-done(((f32[2,256,256]{1,2,0:T(8,128)}), f32[2,256,256]{1,2,0:T(8,128)}) %all-reduce.35.cloned.1.call-update) | async-done | bytes 524304 | tf_op jit(solution)/shard_map/psum | solution.py:14
  866.3 23.7 %custom-call.70 = f32[2,128,128]{2,1,0:T(8,128)S(1)} custom-call(f32[2,128,128]{2,1,0:T(8,128)S(1)} %cholesky.470), custom_call_target="Cholesky" | custom-call | tf_op jit(solution)/shard_map/jit(cholesky)/cholesky | solution.py:47
  910.4 23.5 %custom-call.72 = f32[2,128,128]{2,1,0:T(8,128)S(1)} custom-call(f32[2,128,128]{2,1,0:T(8,128)S(1)} %convolution_subtract_fusion.9), custom_call_target="Cholesky" | custom-call | tf_op jit(solution)/shard_map/jit(cholesky)/cholesky | solution.py:47
  938.3 39.7 %custom-call.73 = f32[2,2,128,128]{2,3,1,0:T(8,128)S(1)} custom-call(f32[2,2,128,128]{3,2,1,0:T(8,128)S(1)} %bitcast.391), custom_call_target="InvertDiagBlocksLowerTriangular" | custom-call | tf_op jit(solution)/shard_map/vmap(jit(_solve_triangular))/triangular_solve | solution.py:48
  991.8 54.5 %all-reduce.37.cloned.1.call-done = f32[2,512,256]{1,2,0:T(8,128)} async-done(((f32[2,512,256]{1,2,0:T(8,128)}), f32[2,512,256]{1,2,0:T(8,128)}) %all-reduce.37.cloned.1.call-update) | async-done | bytes 1048592 | tf_op jit(solution)/shard_map/psum | solution.py:14
  1072.1 74.7 %all-reduce.39.cloned.1.call-done = f32[2,1024,256]{1,2,0:T(8,128)} async-done(((f32[2,1024,256]{1,2,0:T(8,128)}), f32[2,1024,256]{1,2,0:T(8,128)}) %all-reduce.39.cloned.1.call-update) | async-done | bytes 2097168 | tf_op jit(solution)/shard_map/psum | solution.py:14
  1159.9 50.0 %all-reduce.41.cloned.1.call-done = f32[2,256,256]{1,2,0:T(8,128)} async-done(((f32[2,256,256]{1,2,0:T(8,128)}), f32[2,256,256]{1,2,0:T(8,128)}) %all-reduce.41.cloned.1.call-update) | async-done | bytes 524304 | tf_op jit(solution)/shard_map/psum | solution.py:14
  1212.3 23.5 %custom-call.74 = f32[2,128,128]{2,1,0:T(8,128)S(1)} custom-call(f32[2,128,128]{2,1,0:T(8,128)S(1)} %cholesky.473), custom_call_target="Cholesky" | custom-call | tf_op jit(solution)/shard_map/jit(cholesky)/cholesky | solution.py:47
  1256.2 23.5 %custom-call.76 = f32[2,128,128]{2,1,0:T(8,128)S(1)} custom-call(f32[2,128,128]{2,1,0:T(8,128)S(1)} %convolution_subtract_fusion.8), custom_call_target="Cholesky" | custom-call | tf_op jit(solution)/shard_map/jit(cholesky)/cholesky | solution.py:47
  1284.1 39.5 %custom-call.77 = f32[2,2,128,128]{2,3,1,0:T(8,128)S(1)} custom-call(f32[2,2,128,128]{3,2,1,0:T(8,128)S(1)} %bitcast.392), custom_call_target="InvertDiagBlocksLowerTriangular" | custom-call | tf_op jit(solution)/shard_map/vmap(jit(_solve_triangular))/triangular_solve | solution.py:48
  1330.3 61.7 %all-reduce.43.cloned.1.call-done = f32[2,512,256]{1,2,0:T(8,128)} async-done(((f32[2,512,256]{1,2,0:T(8,128)}), f32[2,512,256]{1,2,0:T(8,128)}) %all-reduce.43.cloned.1.call-update) | async-done | bytes 1048592 | tf_op jit(solution)/shard_map/psum | solution.py:14
  1404.4 35.7 %gather_fusion.6 = f32[2048,512]{1,0:T(8,128)} fusion(f32[2,1024,512]{2,1,0:T(8,128)} %copy.472, s32[2048]{0:T(1024)S(1)} %bitcast.375), kind=kCustom, calls=%fused_computation.6 | custom fusion | bytes 8404992 | tf_op jit(solution)/shard_map/vmap(jit(_take))/gather | solution.py:22
  1450.5 20.9 %gather_fusion.7 = f32[1024,1024]{1,0:T(8,128)} fusion(f32[2,512,1024]{2,1,0:T(8,128)} %select_bitcast_fusion.2, s32[1024]{0:T(1024)S(1)} %bitcast.377), kind=kCustom, calls=%fused_computation.7 | custom fusion | bytes 8396800 | tf_op jit(solution)/shard_map/vmap(jit(_take))/gather | solution.py:22
  1564.5 85.5 %gather_fusion.8 = f32[3072,512]{1,0:T(8,128)} fusion(f32[2,1025,512]{2,0,1:T(2,128)} %concatenate.19, s32[3072]{0:T(1024)S(1)} %reshape.1289), kind=kCustom, calls=%fused_computation.8 | custom fusion | bytes 12607488 | tf_op jit(solution)/shard_map/vmap(jit(_take))/gather | solution.py:22
  1676.2 51.1 %gather_fusion.9 = f32[1536,1536]{1,0:T(8,128)} fusion(f32[2,513,1536]{2,0,1:T(2,128)} %concatenate.20, s32[1536]{0:T(1024)S(1)} %reshape.1295), kind=kCustom, calls=%fused_computation.9 | custom fusion | bytes 18886656 | tf_op jit(solution)/shard_map/vmap(jit(_take))/gather | solution.py:22
  1740.4 89.8 %all-reduce.45.cloned.1.call-done = f32[1,1536,256]{1,2,0:T(8,128)} async-done(((f32[1,1536,256]{1,2,0:T(8,128)}), f32[1,1536,256]{1,2,0:T(8,128)}) %all-reduce.45.cloned.1.call-update) | async-done | bytes 1572880 | tf_op jit(solution)/shard_map/psum | solution.py:14
  1832.2 59.8 %all-reduce.47.cloned.1.call-done = f32[1,256,256]{1,2,0:T(8,128)} async-done(((f32[1,256,256]{1,2,0:T(8,128)}), f32[1,256,256]{1,2,0:T(8,128)}) %all-reduce.47.cloned.1.call-update) | async-done | bytes 262160 | tf_op jit(solution)/shard_map/psum | solution.py:14
  1963.7 58.2 %all-reduce.49.cloned.1.call-done = f32[768,256]{0,1:T(8,128)} async-done(((f32[768,256]{0,1:T(8,128)}), f32[768,256]{0,1:T(8,128)}) %all-reduce.49.cloned.1.call-update) | async-done | bytes 786448 | tf_op jit(solution)/shard_map/psum | solution.py:14
  (362 shorter events, 462.5 us)
Async XLA Ops:
  8.0 101.5 %all-reduce.21.cloned.1.call-start = ((), (), s32[]{:S(2)}) async-start(), calls=%async_computation.1 | async-start | bytes 4194304 | tf_op jit(solution)/shard_map/psum | solution.py:14
  16.6 156.0 %all-reduce.23.cloned.1.call-start = ((), (), s32[]{:S(2)}) async-start(), calls=%async_computation.2 | async-start | bytes 1048576 | tf_op jit(solution)/shard_map/psum | solution.py:14
  111.4 243.1 %all-reduce.25.cloned.1.call-start = ((), (), s32[]{:S(2)}) async-start(), calls=%async_computation.3 | async-start | bytes 2097152 | tf_op jit(solution)/shard_map/psum | solution.py:14
  291.1 70.6 %copy-start.4 = (f32[2,1024,256]{1,2,0:T(8,128)}, f32[2,1024,256]{1,2,0:T(8,128)S(1)}, u32[]{:S(2)}) copy-start(f32[2,1024,256]{1,2,0:T(8,128)S(1)} %convolution_select_fusion.4) | copy-start | bytes 6291460
  292.7 162.3 %all-reduce.27.cloned.1.call-start = ((), (), s32[]{:S(2)}) async-start(), calls=%async_computation.4 | async-start | bytes 4194304 | tf_op jit(solution)/shard_map/psum | solution.py:14
  361.7 2.0 copy-start.3
  365.2 152.7 %all-reduce.29.cloned.1.call-start = ((), (), s32[]{:S(2)}) async-start(), calls=%async_computation.5 | async-start | bytes 1048576 | tf_op jit(solution)/shard_map/psum | solution.py:14
  456.9 243.4 %all-reduce.31.cloned.1.call-start = ((), (), s32[]{:S(2)}) async-start(), calls=%async_computation.6 | async-start | bytes 2097152 | tf_op jit(solution)/shard_map/psum | solution.py:14
  636.8 70.7 %copy-start.6 = (f32[2,1024,256]{1,2,0:T(8,128)}, f32[2,1024,256]{1,2,0:T(8,128)S(1)}, u32[]{:S(2)}) copy-start(f32[2,1024,256]{1,2,0:T(8,128)S(1)} %convolution_select_fusion.3) | copy-start | bytes 6291460
  638.5 162.3 %all-reduce.33.cloned.1.call-start = ((), (), s32[]{:S(2)}) async-start(), calls=%async_computation.7 | async-start | bytes 4194304 | tf_op jit(solution)/shard_map/psum | solution.py:14
  707.5 2.0 copy-start.2
  711.0 152.9 %all-reduce.35.cloned.1.call-start = ((), (), s32[]{:S(2)}) async-start(), calls=%async_computation.8 | async-start | bytes 1048576 | tf_op jit(solution)/shard_map/psum | solution.py:14
  802.7 243.6 %all-reduce.37.cloned.1.call-start = ((), (), s32[]{:S(2)}) async-start(), calls=%async_computation.9 | async-start | bytes 2097152 | tf_op jit(solution)/shard_map/psum | solution.py:14
  982.8 70.7 %copy-start.7 = (f32[2,1024,256]{1,2,0:T(8,128)}, f32[2,1024,256]{1,2,0:T(8,128)S(1)}, u32[]{:S(2)}) copy-start(f32[2,1024,256]{1,2,0:T(8,128)S(1)} %convolution_select_fusion.2) | copy-start | bytes 6291460
  982.8 1.7 copy-start.10
  984.5 79.8 %sort.39.cloned.1.call-start = ((), (), s32[]{:S(2)}) async-start(), calls=%async_computation.17 | async-start | bytes 393248 | tf_op jit(solution)/shard_map/jit(argsort)/sort | solution.py:93
  986.2 81.5 %sort.37.cloned.1.call-start = ((), (), s32[]{:S(2)}) async-start(), calls=%async_computation.16 | async-start | bytes 393248 | tf_op jit(solution)/shard_map/jit(argsort)/sort | solution.py:94
  987.5 159.3 %all-reduce.39.cloned.1.call-start = ((), (), s32[]{:S(2)}) async-start(), calls=%async_computation.10 | async-start | bytes 4194304 | tf_op jit(solution)/shard_map/psum | solution.py:14
  1053.5 2.0 copy-start.1
  1057.0 152.9 %all-reduce.41.cloned.1.call-start = ((), (), s32[]{:S(2)}) async-start(), calls=%async_computation.11 | async-start | bytes 1048576 | tf_op jit(solution)/shard_map/psum | solution.py:14
  1148.7 243.2 %all-reduce.43.cloned.1.call-start = ((), (), s32[]{:S(2)}) async-start(), calls=%async_computation.12 | async-start | bytes 2097152 | tf_op jit(solution)/shard_map/psum | solution.py:14
  1328.5 70.4 %copy-start.8 = (f32[2,1024,256]{1,2,0:T(8,128)}, f32[2,1024,256]{1,2,0:T(8,128)S(1)}, u32[]{:S(2)}) copy-start(f32[2,1024,256]{1,2,0:T(8,128)S(1)} %convolution_select_fusion.1) | copy-start | bytes 6291460
  1477.9 61.1 %all-to-all-start = ((f32[128,2,128,32]{2,3,1,0:T(8,128)}), f32[128,2,128,32]{2,3,1,0:T(8,128)}, u32[]{:S(2)}, u32[]{:S(2)}) async-start(f32[128,2,128,32]{2,3,1,0:T(8,128)} %bitcast.384), calls=%async_computation | async-start | bytes 8388608 | tf_op jit(solution)/shard_map/all_to_all | solution.py:127
  1486.5 343.7 %all-reduce.45.cloned.1.call-start = ((), (), s32[]{:S(2)}) async-start(), calls=%async_computation.13 | async-start | bytes 3145728 | tf_op jit(solution)/shard_map/psum | solution.py:14
  1497.6 17.8 copy-start.14
  1497.6 18.2 copy-start.12
  1524.6 9.2 copy-start.13
  1524.6 9.5 copy-start.11
  1731.7 7.4 copy-start
  1740.3 151.7 %all-reduce.47.cloned.1.call-start = ((), (), s32[]{:S(2)}) async-start(), calls=%async_computation.14 | async-start | bytes 524288 | tf_op jit(solution)/shard_map/psum | solution.py:14
  1831.9 190.0 %all-reduce.49.cloned.1.call-start = ((), (), s32[]{:S(2)}) async-start(), calls=%async_computation.15 | async-start | bytes 1572864 | tf_op jit(solution)/shard_map/psum | solution.py:14
  1955.6 5.5 copy-start.5
  (1 other events, 1.1 us)
Sparse Core Ops, SparseCore 0:
  16.7 92.7 all-reduce.20
  112.6 60.0 all-reduce.22
  292.9 61.5 all-reduce.24
  365.4 89.5 all-reduce.26
  457.9 60.0 all-reduce.28
  638.7 61.5 all-reduce.30
  711.2 89.6 all-reduce.32
  803.8 60.0 all-reduce.34
  984.6 61.6 all-reduce.36
  1057.1 89.6 all-reduce.38
  1149.8 60.0 all-reduce.40
  1330.3 61.5 all-reduce.42
  1740.4 89.7 all-reduce.44
  1832.9 59.0 all-reduce.46
  1961.2 60.7 all-reduce.48
Sparse Core Ops, SparseCore 1:
  988.0 6.9 sort.43.cloned.1.call-done
  997.5 9.8 sort.41.cloned.1.call-done
  (2 shorter events, 0.0 us)
where the time goes:
time: 2060 us; the launch traced here: 2050 us
  waiting for transfers between devices  1030 us (50%)
  other arithmetic  548 us (27%)
  local copies, waits for them, and re-layouts  377 us (18%)
  matrix products  67.7 us (3%)
    psum x15, waiting for transfers between devices, from_root(): return lax.psum(kept, axis)  1030 us
    another operation x40, other arithmetic, eliminate(): factor = jnp.linalg.cholesky(corner)  303 us
    gather x8, local copies, waits for them, and re-layouts, take_rows(): jnp.take(single, picks, axis=0)  209 us
    another operation x12, other arithmetic, eliminate(): jax.vmap(partial(jax.scipy.linalg.solve_triangular, lower=True))  179 us
    dot_general x5, matrix products, outer_update(): jnp.einsum('kin,kjn->kij', factor_rows, crossed, precision=exact_mode)  41.4 us
  transfers between devices with their start and end apart: 16, of which 15 were waited for; matrix products, arithmetic and copies ran while one was open for 4% of the time, Pallas kernels for 0%

commit v1 on v0

--- a/solution.py
+++ b/solution.py
@@ -11,7 +11,8 @@
 
 def from_root(value, axis, source):
     kept = jnp.where(lax.axis_index(axis) == source, value, 0).astype(value.dtype)
-    return lax.psum(kept, axis)
+    ladders_store = lambda buf, row_axis: lax.all_gather(buf, axis_name=row_axis).sum(axis=0)
+    return ladders_store(kept, row_axis=axis)
 
 
 def outer_update(factor_rows, crossed):

time: 2060 us -> 2420 us (1.17)
  waiting for transfers between devices: 1030 us -> 1300 us
  other arithmetic: 548 us -> 613 us
    all_gather x0 -> x15, waiting for transfers between devices: none -> 1290 us  [from_root(): lax.all_gather(buf, axis_name=row_axis).sum(axis=0)]
    psum x15 -> x0, waiting for transfers between devices: 1030 us -> none  [from_root(): return lax.psum(kept, axis)]
    unnamed x10 -> x19, other arithmetic: 0.55 us -> 65.2 us
    gather x8 -> x9, local copies, waits for them, and re-layouts: 209 us -> 219 us  [take_rows(): jnp.take(single, picks, axis=0)]
  transfers between devices with their start and end apart: 16 -> 16, of which waited for: 15 -> 16; matrix products, arithmetic and copies ran while one was open for 4% -> 3% of each run, Pallas kernels for 0% -> 0%
where the time goes in v1:
time: 2420 us; the launch traced here: 2400 us
  waiting for transfers between devices  1300 us (54%)
  other arithmetic  613 us (25%)
  local copies, waits for them, and re-layouts  397 us (16%)
  matrix products  58 us (2%)
    all_gather x15, waiting for transfers between devices, from_root(): lax.all_gather(buf, axis_name=row_axis).sum(axis=0)  1290 us
    another operation x40, other arithmetic, eliminate(): factor = jnp.linalg.cholesky(corner)  303 us
    gather x9, local copies, waits for them, and re-layouts, take_rows(): jnp.take(single, picks, axis=0)  219 us
    another operation x12, other arithmetic, eliminate(): jax.vmap(partial(jax.scipy.linalg.solve_triangular, lower=True))  179 us
    unnamed x19, other arithmetic  65.2 us
  transfers between devices with their start and end apart: 16, of which 16 were waited for; matrix products, arithmetic and copies ran while one was open for 3% of the time, Pallas kernels for 0%

profile of v1, /device:TPU:0, one launch (start us, length us, event | category | flops | bytes accessed | tf_op | source)
XLA Modules:
  0.0 2400.5 jit_solution(12774446542400674242)
XLA Ops:
  17.1 199.8 %all-gather.31.cloned.1.call-done = f32[32,1024,256]{2,1,0:T(8,128)} async-done(((f32[2,1024,256]{2,1,0:T(8,128)}), f32[32,1024,256]{2,1,0:T(8,128)}) %all-gather.31.cloned.1.call-update) | async-done | bytes 33554448 | tf_op jit(solution)/shard_map/all_gather | solution.py:14
  230.7 31.7 %all-gather.33.cloned.1.call-done = f32[16,256,256]{2,1,0:T(8,128)} async-done(((f32[2,256,256]{2,1,0:T(8,128)}), f32[16,256,256]{2,1,0:T(8,128)}) %all-gather.33.cloned.1.call-update) | async-done | bytes 4194320 | tf_op jit(solution)/shard_map/all_gather | solution.py:14
  265.2 23.5 custom-call.62
  288.7 19.7 custom-call.63
  309.1 23.5 custom-call.64
  337.1 39.5 %custom-call.65 = f32[2,2,128,128]{2,3,1,0:T(8,128)S(1)} custom-call(f32[2,2,128,128]{3,2,1,0:T(8,128)S(1)} %bitcast.432), custom_call_target="InvertDiagBlocksLowerTriangular" | custom-call | tf_op jit(solution)/shard_map/vmap(jit(_solve_triangular))/triangular_solve | solution.py:49
  383.3 49.8 %all-gather.35.cloned.1.call-done = f32[16,512,256]{2,1,0:T(8,128)} async-done(((f32[2,512,256]{2,1,0:T(8,128)}), f32[16,512,256]{2,1,0:T(8,128)}) %all-gather.35.cloned.1.call-update) | async-done | bytes 8388624 | tf_op jit(solution)/shard_map/all_gather | solution.py:14
  446.8 197.5 %all-gather.37.cloned.1.call-done = f32[32,1024,256]{2,1,0:T(8,128)} async-done(((f32[2,1024,256]{2,1,0:T(8,128)}), f32[32,1024,256]{2,1,0:T(8,128)}) %all-gather.37.cloned.1.call-update) | async-done | bytes 33554448 | tf_op jit(solution)/shard_map/all_gather | solution.py:14
  657.9 31.8 %all-gather.39.cloned.1.call-done = f32[16,256,256]{2,1,0:T(8,128)} async-done(((f32[2,256,256]{2,1,0:T(8,128)}), f32[16,256,256]{2,1,0:T(8,128)}) %all-gather.39.cloned.1.call-update) | async-done | bytes 4194320 | tf_op jit(solution)/shard_map/all_gather | solution.py:14
  692.6 23.7 custom-call.66
  736.7 23.5 custom-call.68
  764.7 39.7 %custom-call.69 = f32[2,2,128,128]{2,3,1,0:T(8,128)S(1)} custom-call(f32[2,2,128,128]{3,2,1,0:T(8,128)S(1)} %bitcast.433), custom_call_target="InvertDiagBlocksLowerTriangular" | custom-call | tf_op jit(solution)/shard_map/vmap(jit(_solve_triangular))/triangular_solve | solution.py:49
  811.2 49.8 %all-gather.41.cloned.1.call-done = f32[16,512,256]{2,1,0:T(8,128)} async-done(((f32[2,512,256]{2,1,0:T(8,128)}), f32[16,512,256]{2,1,0:T(8,128)}) %all-gather.41.cloned.1.call-update) | async-done | bytes 8388624 | tf_op jit(solution)/shard_map/all_gather | solution.py:14
  874.6 197.5 %all-gather.43.cloned.1.call-done = f32[32,1024,256]{2,1,0:T(8,128)} async-done(((f32[2,1024,256]{2,1,0:T(8,128)}), f32[32,1024,256]{2,1,0:T(8,128)}) %all-gather.43.cloned.1.call-update) | async-done | bytes 33554448 | tf_op jit(solution)/shard_map/all_gather | solution.py:14
  1085.8 31.8 %all-gather.45.cloned.1.call-done = f32[16,256,256]{2,1,0:T(8,128)} async-done(((f32[2,256,256]{2,1,0:T(8,128)}), f32[16,256,256]{2,1,0:T(8,128)}) %all-gather.45.cloned.1.call-update) | async-done | bytes 4194320 | tf_op jit(solution)/shard_map/all_gather | solution.py:14
  1120.4 23.6 custom-call.70
  1164.5 23.5 custom-call.72
  1192.6 39.5 %custom-call.73 = f32[2,2,128,128]{2,3,1,0:T(8,128)S(1)} custom-call(f32[2,2,128,128]{3,2,1,0:T(8,128)S(1)} %bitcast.434), custom_call_target="InvertDiagBlocksLowerTriangular" | custom-call | tf_op jit(solution)/shard_map/vmap(jit(_solve_triangular))/triangular_solve | solution.py:49
  1238.7 49.8 %all-gather.47.cloned.1.call-done = f32[16,512,256]{2,1,0:T(8,128)} async-done(((f32[2,512,256]{2,1,0:T(8,128)}), f32[16,512,256]{2,1,0:T(8,128)}) %all-gather.47.cloned.1.call-update) | async-done | bytes 8388624 | tf_op jit(solution)/shard_map/all_gather | solution.py:14
  1302.2 197.5 %all-gather.49.cloned.1.call-done = f32[32,1024,256]{2,1,0:T(8,128)} async-done(((f32[2,1024,256]{2,1,0:T(8,128)}), f32[32,1024,256]{2,1,0:T(8,128)}) %all-gather.49.cloned.1.call-update) | async-done | bytes 33554448 | tf_op jit(solution)/shard_map/all_gather | solution.py:14
  1517.2 28.0 %all-gather.51.cloned.1.call-done = f32[16,256,256]{2,1,0:T(8,128)} async-done(((f32[2,256,256]{2,1,0:T(8,128)}), f32[16,256,256]{2,1,0:T(8,128)}) %all-gather.51.cloned.1.call-update) | async-done | bytes 4194320 | tf_op jit(solution)/shard_map/all_gather | solution.py:14
  1548.0 23.9 custom-call.74
  1592.3 23.5 custom-call.76
  1620.2 39.5 %custom-call.77 = f32[2,2,128,128]{2,3,1,0:T(8,128)S(1)} custom-call(f32[2,2,128,128]{3,2,1,0:T(8,128)S(1)} %bitcast.435), custom_call_target="InvertDiagBlocksLowerTriangular" | custom-call | tf_op jit(solution)/shard_map/vmap(jit(_solve_triangular))/triangular_solve | solution.py:49
  1732.8 35.6 %gather_fusion.6 = f32[2048,512]{1,0:T(8,128)} fusion(f32[2,1024,512]{2,1,0:T(8,128)} %copy.494, s32[2048]{0:T(1024)S(1)} %bitcast.399), kind=kCustom, calls=%fused_computation.6 | custom fusion | bytes 8404992 | tf_op jit(solution)/shard_map/vmap(jit(_take))/gather | solution.py:23
  1778.9 21.3 gather_fusion.7
  1892.4 85.6 %gather_fusion.8 = f32[3072,512]{1,0:T(8,128)} fusion(f32[2,1025,512]{2,0,1:T(2,128)} %concatenate.19, s32[3072]{0:T(1024)S(1)} %reshape.1288), kind=kCustom, calls=%fused_computation.8 | custom fusion | bytes 12607488 | tf_op jit(solution)/shard_map/vmap(jit(_take))/gather | solution.py:23
  2004.2 51.1 %gather_fusion.9 = f32[1536,1536]{1,0:T(8,128)} fusion(f32[2,513,1536]{2,0,1:T(2,128)} %concatenate.20, s32[1536]{0:T(1024)S(1)} %reshape.1294), kind=kCustom, calls=%fused_computation.9 | custom fusion | bytes 18886656 | tf_op jit(solution)/shard_map/vmap(jit(_take))/gather | solution.py:23
  2077.6 151.6 %all-gather.55.cloned.1.call-done = f32[16,1536,256]{2,1,0:T(8,128)} async-done(((f32[1,1536,256]{2,1,0:T(8,128)}), f32[16,1536,256]{2,1,0:T(8,128)}) %all-gather.55.cloned.1.call-update) | async-done | bytes 25165840 | tf_op jit(solution)/shard_map/all_gather | solution.py:14
  2239.7 24.6 %all-gather.57.cloned.1.call-done = f32[8,256,256]{2,1,0:T(8,128)} async-done(((f32[1,256,256]{2,1,0:T(8,128)}), f32[8,256,256]{2,1,0:T(8,128)}) %all-gather.57.cloned.1.call-update) | async-done | bytes 2097168 | tf_op jit(solution)/shard_map/all_gather | solution.py:14
  2309.5 20.5 custom-call.33
  2338.8 38.7 %all-gather.59.cloned.1.call-done = f32[6144,256]{0,1:T(8,128)} async-done(((f32[768,256]{0,1:T(8,128)}), f32[6144,256]{0,1:T(8,128)}) %all-gather.59.cloned.1.call-update) | async-done | bytes 6291472 | tf_op jit(solution)/shard_map/all_gather | solution.py:14
  (415 shorter events, 542.7 us)
Async XLA Ops:
  8.0 208.9 %all-gather.31.cloned.1.call-start = ((), (), s32[]{:S(2)}) async-start(), calls=%async_computation.1 | async-start | bytes 35651584 | tf_op jit(solution)/shard_map/all_gather | solution.py:14
  17.0 245.3 %all-gather.33.cloned.1.call-start = ((), (), s32[]{:S(2)}) async-start(), calls=%async_computation.2 | async-start | bytes 4718592 | tf_op jit(solution)/shard_map/all_gather | solution.py:14
  229.0 35.9 %copy-start.10 = (f32[2,1024,256]{2,1,0:T(8,128)}, f32[2,1024,256]{2,1,0:T(8,128)S(1)}, u32[]{:S(2)}) copy-start(f32[2,1024,256]{2,1,0:T(8,128)S(1)} %reduce_sum.139) | copy-start | bytes 6291460
  230.5 202.6 %all-gather.35.cloned.1.call-start = ((), (), s32[]{:S(2)}) async-start(), calls=%async_computation.3 | async-start | bytes 9437184 | tf_op jit(solution)/shard_map/all_gather | solution.py:14
  381.4 55.7 %copy-start.4 = (f32[2,1024,256]{1,2,0:T(8,128)}, f32[2,1024,256]{1,2,0:T(8,128)S(1)}, u32[]{:S(2)}) copy-start(f32[2,1024,256]{1,2,0:T(8,128)S(1)} %convolution_select_fusion.4) | copy-start | bytes 6291460
  383.3 261.0 %all-gather.37.cloned.1.call-start = ((), (), s32[]{:S(2)}) async-start(), calls=%async_computation.4 | async-start | bytes 35651584 | tf_op jit(solution)/shard_map/all_gather | solution.py:14
  446.7 243.0 %all-gather.39.cloned.1.call-start = ((), (), s32[]{:S(2)}) async-start(), calls=%async_computation.5 | async-start | bytes 4718592 | tf_op jit(solution)/shard_map/all_gather | solution.py:14
  656.3 35.9 %copy-start.11 = (f32[2,1024,256]{2,1,0:T(8,128)}, f32[2,1024,256]{2,1,0:T(8,128)S(1)}, u32[]{:S(2)}) copy-start(f32[2,1024,256]{2,1,0:T(8,128)S(1)} %reduce_sum.142) | copy-start | bytes 6291460
  657.8 203.1 %all-gather.41.cloned.1.call-start = ((), (), s32[]{:S(2)}) async-start(), calls=%async_computation.6 | async-start | bytes 9437184 | tf_op jit(solution)/shard_map/all_gather | solution.py:14
  809.3 55.8 %copy-start.6 = (f32[2,1024,256]{1,2,0:T(8,128)}, f32[2,1024,256]{1,2,0:T(8,128)S(1)}, u32[]{:S(2)}) copy-start(f32[2,1024,256]{1,2,0:T(8,128)S(1)} %convolution_select_fusion.3) | copy-start | bytes 6291460
  811.1 261.0 %all-gather.43.cloned.1.call-start = ((), (), s32[]{:S(2)}) async-start(), calls=%async_computation.7 | async-start | bytes 35651584 | tf_op jit(solution)/shard_map/all_gather | solution.py:14
  874.6 243.0 %all-gather.45.cloned.1.call-start = ((), (), s32[]{:S(2)}) async-start(), calls=%async_computation.8 | async-start | bytes 4718592 | tf_op jit(solution)/shard_map/all_gather | solution.py:14
  1084.2 35.9 %copy-start.12 = (f32[2,1024,256]{2,1,0:T(8,128)}, f32[2,1024,256]{2,1,0:T(8,128)S(1)}, u32[]{:S(2)}) copy-start(f32[2,1024,256]{2,1,0:T(8,128)S(1)} %reduce_sum.145) | copy-start | bytes 6291460
  1085.7 202.8 %all-gather.47.cloned.1.call-start = ((), (), s32[]{:S(2)}) async-start(), calls=%async_computation.9 | async-start | bytes 9437184 | tf_op jit(solution)/shard_map/all_gather | solution.py:14
  1236.9 55.7 %copy-start.7 = (f32[2,1024,256]{1,2,0:T(8,128)}, f32[2,1024,256]{1,2,0:T(8,128)S(1)}, u32[]{:S(2)}) copy-start(f32[2,1024,256]{1,2,0:T(8,128)S(1)} %convolution_select_fusion.2) | copy-start | bytes 6291460
  1238.7 261.0 %all-gather.49.cloned.1.call-start = ((), (), s32[]{:S(2)}) async-start(), calls=%async_computation.10 | async-start | bytes 35651584 | tf_op jit(solution)/shard_map/all_gather | solution.py:14
  1302.1 243.0 %all-gather.51.cloned.1.call-start = ((), (), s32[]{:S(2)}) async-start(), calls=%async_computation.11 | async-start | bytes 4718592 | tf_op jit(solution)/shard_map/all_gather | solution.py:14
  1513.3 159.5 %sort.39.cloned.1.call-start = ((), (), s32[]{:S(2)}) async-start(), calls=%async_computation.17 | async-start | bytes 393248 | tf_op jit(solution)/shard_map/jit(argsort)/sort | solution.py:94
  1515.8 175.6 %sort.37.cloned.1.call-start = ((), (), s32[]{:S(2)}) async-start(), calls=%async_computation.16 | async-start | bytes 393248 | tf_op jit(solution)/shard_map/jit(argsort)/sort | solution.py:95
  1517.1 199.1 %all-gather.53.cloned.1.call-start = ((), (), s32[]{:S(2)}) async-start(), calls=%async_computation.12 | async-start | bytes 9437184 | tf_op jit(solution)/shard_map/all_gather | solution.py:14
  1664.6 55.7 %copy-start.8 = (f32[2,1024,256]{1,2,0:T(8,128)}, f32[2,1024,256]{1,2,0:T(8,128)S(1)}, u32[]{:S(2)}) copy-start(f32[2,1024,256]{1,2,0:T(8,128)S(1)} %convolution_select_fusion.1) | copy-start | bytes 6291460
  1778.9 21.4 copy-start.16
  1806.8 60.1 %all-to-all-start = ((f32[128,2,128,32]{2,3,1,0:T(8,128)}), f32[128,2,128,32]{2,3,1,0:T(8,128)}, u32[]{:S(2)}, u32[]{:S(2)}) async-start(f32[128,2,128,32]{2,3,1,0:T(8,128)} %bitcast.416), calls=%async_computation | async-start | bytes 8388608 | tf_op jit(solution)/shard_map/all_to_all | solution.py:128
  1816.1 413.1 %all-gather.55.cloned.1.call-start = ((), (), s32[]{:S(2)}) async-start(), calls=%async_computation.13 | async-start | bytes 26738688 | tf_op jit(solution)/shard_map/all_gather | solution.py:14
  1834.2 18.4 copy-start.18
  1834.2 18.7 copy-start.20
  2077.6 186.7 %all-gather.57.cloned.1.call-start = ((), (), s32[]{:S(2)}) async-start(), calls=%async_computation.14 | async-start | bytes 2359296 | tf_op jit(solution)/shard_map/all_gather | solution.py:14
  2238.5 49.7 %copy-start.15 = (f32[1536,256]{1,0:T(8,128)}, f32[1536,256]{1,0:T(8,128)S(1)}, u32[]{:S(2)}) copy-start(f32[1536,256]{1,0:T(8,128)S(1)} %reduce.33) | copy-start | bytes 4718596
  2239.4 138.2 %all-gather.59.cloned.1.call-start = ((), (), s32[]{:S(2)}) async-start(), calls=%async_computation.15 | async-start | bytes 7077888 | tf_op jit(solution)/shard_map/all_gather | solution.py:14
  2266.4 21.8 copy-start.17
  2288.2 48.0 %copy-start.5 = (f32[2,1024,256]{1,2,0:T(8,128)S(1)}, f32[2,1024,256]{1,2,0:T(8,128)}, u32[]{:S(2)}) copy-start(f32[2,1024,256]{1,2,0:T(8,128)} %copy-done.4) | copy-start | bytes 6291460
  2336.2 48.5 %slice-start = ((s8[9437184]{0:T(1024)(128)(4,1)}), s8[1048576]{0:T(1024)(128)(4,1)S(1)}, s32[]{:S(2)}) async-start(s8[9437184]{0:T(1024)(128)(4,1)} %bitcast.403), calls=%async_computation.20 | async-start | bytes 2097152
  (13 other events, 84.8 us)
Sparse Core Ops, SparseCore 0:
  17.2 199.6 all-gather.30
  230.6 31.7 all-gather.32
  383.4 49.6 all-gather.34
  446.8 197.3 all-gather.36
  658.0 31.7 all-gather.38
  811.3 49.6 all-gather.40
  874.7 197.3 all-gather.42
  1085.8 31.7 all-gather.44
  1238.8 49.6 all-gather.46
  1302.3 197.3 all-gather.48
  1513.4 31.7 all-gather.50
  1666.5 49.6 all-gather.52
  2077.7 151.4 all-gather.54
  2239.5 24.7 all-gather.56
  2336.3 41.2 all-gather.58
Sparse Core Ops, SparseCore 1:
  1516.8 7.0 sort.43.cloned.1.call-done
  1526.3 9.7 sort.41.cloned.1.call-done
  (2 shorter events, 0.0 us)
